TPU v7x, 32 devices: a whole 2x2x4 slice. The times are simulated.
32 devices in a mesh: dp: 4 (over z), tensor: 8 (over y, x, core).
Axes of the slice: x: 2, y: 2, z: 4, core: 2. Of those that a mesh axis runs over, the one named last changes fastest.
Arguments:
- teacher_hidden: bfloat16 [64, 5120], P('dp', 'tensor'), may hold values from -200 to 200
- student_hidden: bfloat16 [64, 4096], P('dp', 'tensor'), may hold values from -8 to 8
- teacher_head: bfloat16 [5120, 8192], P(None, ('dp', 'tensor')), may hold values from -6 to 6
- student_head: bfloat16 [4096, 8192], P(None, ('dp', 'tensor')), may hold values from -6 to 6
- teacher_gain: float32 [5120], replicated, may hold values from 0.5 to 1.5
- lengths: int32 [8], replicated, may hold values from 1 to 8, as said below
- student_row: int32 [64], replicated, may hold values from 0 to 63, as said below
- targets: int32 [64], replicated, may hold values from 0 to 8191
Outputs:
- grad_logits: bfloat16 [64, 8192], P(None, ('dp', 'tensor'))
- divergence: float32 [64], P('dp')
- log_ratio: float32 [64], P('dp')
Inputs may be any that keep to these rules, and one draw needn't show every extreme that they name: The lengths of the 2 responses of one index of dp sum to at most 8, and to exactly 8 on some index. `student_row`: a permutation: every row of student_hidden is named once.
All inputs are finite; a program needn't handle non-finite values.
Results may differ from a plain program's by a relative error of at most 0.01095.
Values may be sent and summed in bfloat16 or wider, within the bound.
A program may use at most 64 MiB of HBM per device.

v0:
```python
import jax
import jax.numpy as jnp
from jax import lax
from jax.sharding import PartitionSpec as P

SLOT = 8


def merged_2(array, axis, combine):
    everything = jax.tree.map(lambda part: lax.all_gather(part, axis), array)
    initial = jax.tree.map(lambda part: part[0], everything)

    def turn(k, so_far):
        return combine(so_far, jax.tree.map(lambda part: part[k], everything))

    return lax.fori_loop(1, lax.axis_size(axis), turn, initial)


def on_device(
    teacher_hidden,
    student_hidden,
    teacher_head,
    student_head,
    teacher_gain,
    lengths,
    student_row,
    targets,
):
    dp_count = lax.axis_size("dp")
    tensor_count = lax.axis_size("tensor")
    local_tokens = teacher_hidden.shape[0]
    token_count = local_tokens * dp_count
    vocab_local = teacher_head.shape[1]
    dp_index = lax.axis_index("dp")
    vocab_start = (dp_index * tensor_count + lax.axis_index("tensor")) * vocab_local
    token_ids = jnp.arange(token_count, dtype=jnp.int32)
    live_all = (token_ids % SLOT < lengths[token_ids // SLOT]).astype(jnp.float32)
    teacher_full, student_full = (
        lax.all_gather(teacher_hidden, "tensor", axis=1, tiled=True),
        lax.all_gather(student_hidden, "tensor", axis=1, tiled=True),
    )
    values = lax.all_gather(teacher_full, "dp", axis=0, tiled=True).astype(jnp.float32)
    row_scale = lax.rsqrt(jnp.mean(values * values, axis=1, keepdims=True) + 1e-06)
    normed = (values * row_scale * teacher_gain[None, :]).astype(jnp.bfloat16)
    teacher_logits = jnp.dot(normed, teacher_head, preferred_element_type=jnp.float32)
    student_all = lax.all_gather(student_full, "dp", axis=0, tiled=True)
    chosen_rows = student_all[student_row[token_ids]]
    student_logits = jnp.dot(chosen_rows, student_head, preferred_element_type=jnp.float32)
    target_local = targets[token_ids] - vocab_start
    target_hits = (
        target_local[:, None] == jnp.arange(vocab_local, dtype=jnp.int32)[None, :]
    ).astype(jnp.float32)
    target_teacher = jnp.sum(target_hits * teacher_logits, axis=1)
    target_student = jnp.sum(target_hits * student_logits, axis=1)
    teacher_max = jnp.max(teacher_logits, axis=1)
    student_max = jnp.max(student_logits, axis=1)
    teacher_exp = jnp.exp(teacher_logits - teacher_max[:, None])
    student_exp = jnp.exp(student_logits - student_max[:, None])
    cross_sum = jnp.sum(student_exp * (student_logits - teacher_logits), axis=1)

    def combine(earlier, later):
        top_teacher = jnp.maximum(earlier[0], later[0])
        teacher_total = earlier[1] * jnp.exp(earlier[0] - top_teacher) + later[1] * jnp.exp(
            later[0] - top_teacher
        )
        top_student = jnp.maximum(earlier[2], later[2])
        early_rescale = jnp.exp(earlier[2] - top_student)
        late_rescale = jnp.exp(later[2] - top_student)
        return (
            top_teacher,
            teacher_total,
            top_student,
            earlier[3] * early_rescale + later[3] * late_rescale,
            earlier[4] * early_rescale + later[4] * late_rescale,
            earlier[5] + later[5],
            earlier[6] + later[6],
        )

    merged = merged_2(
        (
            teacher_max,
            jnp.sum(teacher_exp, axis=1),
            student_max,
            jnp.sum(student_exp, axis=1),
            cross_sum,
            target_teacher,
            target_student,
        ),
        ("dp", "tensor"),
        combine,
    )
    teacher_lse = merged[0] + jnp.log(merged[1])
    student_lse = merged[2] + jnp.log(merged[3])
    teacher_logp = teacher_logits - teacher_lse[:, None]
    student_logp = student_logits - student_lse[:, None]
    student_prob = jnp.exp(student_logp)
    kl_raw = merged[4] / merged[3] - student_lse + teacher_lse
    picked_teacher = merged[5]
    picked_student = merged[6]
    gradient = (
        live_all[:, None] * student_prob * (student_logp - teacher_logp - kl_raw[:, None])
    ).astype(jnp.bfloat16)
    kl_rows = live_all * kl_raw
    ratio_rows = live_all * (picked_student - student_lse - (picked_teacher - teacher_lse))
    divergence = lax.dynamic_slice_in_dim(kl_rows, dp_index * local_tokens, local_tokens)
    log_ratio = lax.dynamic_slice_in_dim(ratio_rows, dp_index * local_tokens, local_tokens)
    return (gradient, divergence, log_ratio)


def solution(mesh):
    return jax.shard_map(
        on_device,
        mesh=mesh,
        in_specs=(
            P("dp", "tensor"),
            P("dp", "tensor"),
            P(None, ("dp", "tensor")),
            P(None, ("dp", "tensor")),
            P(),
            P(),
            P(),
            P(),
        ),
        out_specs=(P(None, ("dp", "tensor")), P("dp"), P("dp")),
        check_vma=False,
    )
```

profile of v0, /device:TPU:0, one launch (start us, length us, event | category | flops | bytes accessed | tf_op | source)
XLA Modules:
  0.0 115.9 jit_solution(16936663235237315496)
XLA Ops:
  0.7 1.6 %gather_fusion.2 = s32[64]{0:T(128)S(1)} fusion(s32[64]{0:T(128)} %param.17, s32[1024]{0:T(1024)S(1)} %pad_clamp_fusion.1), kind=kCustom, calls=%fused_computation.2 | custom fusion | bytes 768 | tf_op jit(solution)/shard_map/gather | solution.py:49
  2.3 11.0 %all_gather.56 = bf16[16,5120]{1,0:T(8,128)(2,1)S(1)} all-gather(bf16[16,640]{1,0:T(8,128)(2,1)} %param.10), channel_id=1, replica_groups=mesh['dp'=4,'tensor'=8] {'tensor'}, dimensions={1}, use_global_device_ids=true | all-gather | bytes 184320 | tf_op jit(solution)/shard_map/all_gather | solution.py:39
  13.2 18.4 %all_gather.57 = bf16[64,5120]{1,0:T(8,128)(2,1)S(1)} all-gather(bf16[16,5120]{1,0:T(8,128)(2,1)S(1)} %all_gather.56), channel_id=1, replica_groups=mesh['dp'=4,'tensor'=8] {'dp'}, dimensions={0}, use_global_device_ids=true | all-gather | bytes 819200 | tf_op jit(solution)/shard_map/all_gather | solution.py:42
  31.6 0.2 fusion.17
  31.9 0.7 fusion.32
  32.6 0.8 gather_fusion
  33.4 9.0 %all_gather.54 = bf16[16,4096]{1,0:T(8,128)(2,1)S(1)} all-gather(bf16[16,512]{1,0:T(8,128)(2,1)S(1)} %copy-done.4), channel_id=1, replica_groups=mesh['dp'=4,'tensor'=8] {'tensor'}, dimensions={1}, use_global_device_ids=true | all-gather | bytes 147456 | tf_op jit(solution)/shard_map/all_gather | solution.py:40
  42.4 15.5 %all_gather.55 = bf16[64,4096]{1,0:T(8,128)(2,1)S(1)} all-gather(bf16[16,4096]{1,0:T(8,128)(2,1)S(1)} %all_gather.54), channel_id=1, replica_groups=mesh['dp'=4,'tensor'=8] {'dp'}, dimensions={0}, use_global_device_ids=true | all-gather | bytes 655360 | tf_op jit(solution)/shard_map/all_gather | solution.py:46
  57.9 1.7 %gather_fusion.1 = bf16[64,4096]{1,0:T(8,128)(2,1)} fusion(bf16[64,4096]{1,0:T(8,128)(2,1)S(1)} %all_gather.55, s32[1024]{0:T(1024)S(1)} %pad_clamp_fusion), kind=kCustom, calls=%fused_computation.1 | custom fusion | bytes 1048832 | tf_op jit(solution)/shard_map/gather | solution.py:47
  59.6 2.3 %fusion.33 = (f32[64]{0:T(128)S(1)}, f32[64,256]{1,0:T(8,128)S(1)}) fusion(bf16[64,4096]{1,0:T(8,128)(2,1)} %gather_fusion.1, bf16[4096,256]{1,0:T(8,128)(2,1)} %param.13), kind=kOutput, calls=%fused_computation.73 | convolution fusion | flops 134234048 | bytes 2687232 | tf_op jit(solution)/shard_map/dot_general | solution.py:48
  61.9 0.3 multiply_reduce_fusion
  62.2 0.3 dynamic-update-slice.3
  62.5 0.3 dynamic-update-slice.4
  62.8 0.3 dynamic-update-slice.5
  63.0 0.3 dynamic-update-slice.6
  63.3 0.3 dynamic-update-slice.1
  63.6 0.3 dynamic-update-slice
  63.8 0.3 dynamic-update-slice.2
  64.1 40.1 %all-reduce.7 = (f32[2048]{0:T(1024)S(1)}, f32[2048]{0:T(1024)S(1)}, f32[2048]{0:T(1024)S(1)}, f32[2048]{0:T(1024)S(1)}, f32[2048]{0:T(1024)S(1)}, /*index=5*/f32[2048]{0:T(1024)S(1)}, f32[2048]{0:T(1024)S(1)}) all-reduce(f32[2048]{0:T(1024)S(1)} %dynamic-update-slice, ...), channel_id=2, replica_groups=mesh['dp'=4,'tensor'=8] {'dp','tensor'}, use_global_device_ids=true, to_apply=%add | all-reduce | flops 14336 | bytes 114688
  104.2 0.1 reshape.131
  104.3 0.1 reshape.132
  104.3 0.1 reshape.133
  104.4 0.1 reshape.134
  104.5 0.1 reshape.135
  104.5 0.1 reshape.136
  104.6 0.1 reshape.137
  104.7 3.5 %while.27 = (s32[]{:T(128)}, f32[64]{0:T(128)S(1)}, f32[64]{0:T(128)S(1)}, f32[64]{0:T(128)S(1)}, f32[64]{0:T(128)S(1)}, /*index=5*/f32[64]{0:T(128)S(1)}, f32[6...) while((s32[]{:T(128)}, f32[64]{0:T(128)S(1)}, ...), condition=%wide.region_9.10_spmd, body=%wide.region_8.9_spmd.sunk | while | flops 1221 | bytes 6875 | solution.py:16
  108.2 0.7 fusion.31
  108.9 5.1 %subtract_select_fusion = (f32[64]{0:T(128)S(1)}, pred[64]{0:T(512)(128)(4,1)S(1)}, f32[64]{0:T(128)S(1)}, f32[64]{0:T(128)S(1)}) fusion(f32[64]{0:T(128)S(1)} %get-tuple-element.367, f32[64]{0:T(128)S(1)} %get-tuple-element.366, s32[]{:T(128)} %bitcast.15, s32[]{:T(128)} %bitcast.14, s32[]{:T(128)} %bitcast.13, s32[]{:T(128)} %bitcast.12, s32[]{:T(128)} %bitcast.11, ...), kind=kLoop, calls=%fused_computation.64 | loop fusion | flops 2432 | bytes 2400 | tf_op jit(solution)/shard_map/mul | solution.py:104
  114.0 0.7 multiply_convert_fusion
  114.7 0.6 dynamic_slice.76
  115.3 0.6 dynamic_slice.77
  (156 shorter events, 2.5 us)
Async XLA Ops:
  0.6 31.2 %copy-start = (bf16[5120,256]{1,0:T(8,128)(2,1)S(1)}, bf16[5120,256]{1,0:T(8,128)(2,1)}, u32[]{:S(2)}) copy-start(bf16[5120,256]{1,0:T(8,128)(2,1)} %param.12) | copy-start | bytes 7864324
  0.6 31.2 %copy-start.3 = (f32[5120]{0:T(1024)S(1)}, f32[5120]{0:T(1024)}, u32[]{:S(2)}) copy-start(f32[5120]{0:T(1024)} %param.14) | copy-start | bytes 61444
  31.6 1.0 copy-start.1
  31.8 1.6 %copy-start.4 = (bf16[16,512]{1,0:T(8,128)(2,1)S(1)}, bf16[16,512]{1,0:T(8,128)(2,1)}, u32[]{:S(2)}) copy-start(bf16[16,512]{1,0:T(8,128)(2,1)} %param.11) | copy-start | bytes 49156
  59.6 48.6 %copy-start.2 = (s32[8]{0:T(128)S(1)}, s32[8]{0:T(128)}, u32[]{:S(2)}) copy-start(s32[8]{0:T(128)} %param.15) | copy-start | bytes 100
where the time goes:
time: 116 us
  blocking collectives  94 us (81%)
  other arithmetic  8.71 us (8%)
  local copies, waits for them, and re-layouts  8.31 us (7%)
  matrix products  3.05 us (3%)
    unnamed x1, blocking collectives  40.1 us
    all_gather x1, blocking collectives, on_device(): lax.all_gather(teacher_full, 'dp', axis=0, tiled=True).astype(jnp.float32)  18.4 us
    all_gather x1, blocking collectives, on_device(): student_all = lax.all_gather(student_full, 'dp', axis=0, tiled=True)  15.5 us
    all_gather x1, blocking collectives, on_device(): lax.all_gather(teacher_hidden, 'tensor', axis=1, tiled=True)  11 us
    all_gather x1, blocking collectives, on_device(): lax.all_gather(student_hidden, 'tensor', axis=1, tiled=True)  9.03 us
    mul x1, other arithmetic, on_device(): live_all * (picked_student - student_lse - (picked_teacher - teacher_lse))  5.07 us
    gather x2, local copies, waits for them, and re-layouts, on_device(): chosen_rows = student_all[student_row[token_ids]]  2.44 us
    dot_general x1, matrix products, on_device(): jnp.dot(chosen_rows, student_head, preferred_element_type=jnp.float32)  2.34 us

commit v1 on v0

v1 whole, which is shorter than its diff:
```python
import functools

import jax
import jax.numpy as jnp
from jax import lax
from jax.experimental import pallas as pl
from jax.experimental.pallas import tpu as pltpu
from jax.sharding import PartitionSpec as P

LIVE = 8
MESH = pl.DeviceIdType.MESH


def kernel(
    n_dp,
    n_t,
    th_hbm,
    sh_hbm,
    thead_hbm,
    shead_hbm,
    gain_hbm,
    len_hbm,
    srow_hbm,
    tgt_hbm,
    out_ref,
    div_ref,
    ratio_ref,
    th,
    thead,
    shead,
    gain,
    lens,
    srow,
    tgt,
    tg,
    sz,
    sg,
    mine,
    stats,
    local_sem,
    zt_send,
    zt_recv,
    zs_send,
    zs_recv,
    xt_send,
    xt_recv,
    xs_send,
    xs_recv,
    pt_send,
    pt_recv,
    ps_send,
    ps_recv,
    st_send,
    st_recv,
):
    f32, bf16 = jnp.float32, jnp.bfloat16
    d = lax.axis_index("dp")
    t = lax.axis_index("tensor")
    half = n_t // 2
    chip, core = t // 2, t % 2
    partner = chip * 2 + 1 - core
    local_tokens, width_t = th_hbm.shape
    width_s = sh_hbm.shape[1]
    tokens = local_tokens * n_dp
    seqs = lens.shape[0]
    seq_dev = seqs // n_dp
    slot = tokens // seqs
    vocab = thead.shape[1]
    rows = n_dp * LIVE
    lanes = 4 * rows
    n_dev = n_dp * n_t

    local = [
        pltpu.make_async_copy(src, dst, local_sem.at[i])
        for i, (src, dst) in enumerate(
            [
                (len_hbm, lens),
                (th_hbm, th),
                (sh_hbm, sz.at[d]),
                (srow_hbm, srow),
                (tgt_hbm, tgt),
                (gain_hbm, gain),
                (shead_hbm, shead),
                (thead_hbm, thead),
            ]
        )
    ]
    for copy in local:
        copy.start()

    def dp_peer(k):
        return lax.rem(d + k, n_dp)

    def chip_peer(k):
        return lax.rem(chip + k, half) * 2 + core

    barrier = pltpu.get_barrier_semaphore()
    for k in range(1, n_dp):
        pl.semaphore_signal(barrier, inc=1, device_id=(dp_peer(k), t), device_id_type=MESH)
    for k in range(1, half):
        pl.semaphore_signal(barrier, inc=1, device_id=(d, chip_peer(k)), device_id_type=MESH)
    pl.semaphore_signal(barrier, inc=1, device_id=(d, partner), device_id_type=MESH)

    local[0].wait()
    lane = lax.broadcasted_iota(jnp.int32, (1, local_tokens), 1)
    own_slot = jnp.full((1, local_tokens), -1, jnp.int32)
    offset = jnp.int32(0)
    for q in range(seq_dev):
        length = lens[d * seq_dev + q]
        pos = lane - q * slot
        own_slot = jnp.where((pos >= 0) & (pos < length), pos + offset, own_slot)
        offset = offset + length
    own_hit = lax.broadcasted_iota(jnp.int32, (LIVE, local_tokens), 0) == own_slot
    local[1].wait()
    tg[t, d] = jnp.dot(
        jnp.where(own_hit, 1.0, 0.0).astype(bf16), th[...], preferred_element_type=f32
    ).astype(bf16)
    local[2].wait()

    pl.semaphore_wait(barrier, n_dp - 1 + half - 1 + 1)

    def remote(src, dst, send, recv, device):
        return pltpu.make_async_remote_copy(
            src_ref=src, dst_ref=dst, send_sem=send, recv_sem=recv, device_id=device, device_id_type=MESH
        )

    started = []
    z_t, z_s = [], []
    for k in range(1, n_dp):
        z_t.append(
            remote(tg.at[t, d], tg.at[t, d], zt_send.at[k], zt_recv.at[k], (dp_peer(k), t))
        )
        z_s.append(remote(sz.at[d], sz.at[d], zs_send.at[k], zs_recv.at[k], (dp_peer(k), t)))
    for copy in z_t + z_s:
        copy.start()
    started += z_t + z_s

    local[3].wait()
    local[4].wait()
    token = lax.broadcasted_iota(jnp.int32, (1, tokens), 1)
    slot_of = jnp.full((1, tokens), -1, jnp.int32)
    for s in range(seqs):
        if s % seq_dev == 0:
            offset = jnp.int32(s // seq_dev * LIVE)
        length = lens[s]
        pos = token - s * slot
        slot_of = jnp.where((pos >= 0) & (pos < length), pos + offset, slot_of)
        offset = offset + length
    row = lax.broadcasted_iota(jnp.int32, (rows, tokens), 0)
    hit = row == slot_of
    hit_bf16 = jnp.where(hit, 1.0, 0.0).astype(bf16)
    source = jnp.sum(jnp.where(hit, srow[...].astype(f32), 0.0), axis=1, keepdims=True)
    wanted = jnp.sum(jnp.where(hit, tgt[...].astype(f32), 0.0), axis=1, keepdims=True)
    pick = lax.broadcasted_iota(jnp.int32, (rows, tokens), 1) == source.astype(jnp.int32)
    pick_bf16 = jnp.where(pick, 1.0, 0.0).astype(bf16)

    for copy in z_t:
        copy.wait_recv()
    x_t = [
        remote(tg.at[t], tg.at[t], xt_send.at[k], xt_recv.at[k], (d, chip_peer(k)))
        for k in range(1, half)
    ]
    p_t = [remote(tg.at[t], tg.at[t], pt_send.at[0], pt_recv.at[0], (d, partner))]
    for copy in x_t + p_t:
        copy.start()

    for copy in z_s:
        copy.wait_recv()
    everyone = sz[...].reshape(tokens, width_s)
    sg[t] = jnp.dot(pick_bf16, everyone, preferred_element_type=f32).astype(bf16)
    x_s = [
        remote(sg.at[t], sg.at[t], xs_send.at[k], xs_recv.at[k], (d, chip_peer(k)))
        for k in range(1, half)
    ]
    p_s = [remote(sg.at[t], sg.at[t], ps_send.at[0], ps_recv.at[0], (d, partner))]
    for copy in x_s + p_s:
        copy.start()

    for copy in local[5:]:
        copy.wait()

    square = jnp.zeros((rows, 1), f32)
    acc_t = jnp.zeros((2 * rows, vocab), f32)
    acc_s = jnp.zeros((rows, vocab), f32)

    def add(which, square, acc_t, acc_s):
        x = tg[which].astype(f32).reshape(rows, width_t)
        square = square + jnp.sum(x * x, axis=1, keepdims=True)
        x = x * gain[which]
        high = x.astype(bf16)
        low = (x - high.astype(f32)).astype(bf16)
        at_t = pl.ds(pl.multiple_of(which * width_t, width_t), width_t)
        at_s = pl.ds(pl.multiple_of(which * width_s, width_s), width_s)
        acc_t = acc_t + jnp.dot(
            jnp.concatenate([high, low], axis=0), thead[at_t, :], preferred_element_type=f32
        )
        acc_s = acc_s + jnp.dot(sg[which], shead[at_s, :], preferred_element_type=f32)
        return square, acc_t, acc_s

    sums = add(t, square, acc_t, acc_s)
    for k in range(1, half):
        origin = lax.rem(chip - k + half, half) * 2 + core
        x_t[k - 1].wait_recv()
        copy = remote(tg.at[origin], tg.at[origin], pt_send.at[k], pt_recv.at[k], (d, partner))
        copy.start()
        p_t.append(copy)
        x_s[k - 1].wait_recv()
        copy = remote(sg.at[origin], sg.at[origin], ps_send.at[k], ps_recv.at[k], (d, partner))
        copy.start()
        p_s.append(copy)
        sums = add(origin, *sums)
    for k in range(half):
        origin = lax.rem(chip - k + half, half) * 2 + 1 - core
        p_t[k].wait_recv()
        p_s[k].wait_recv()
        sums = add(origin, *sums)
    square, acc_t, acc_s = sums
    started += x_t + x_s + p_t + p_s

    scale = lax.rsqrt(square / (width_t * n_t) + 1e-06)
    logits_t = (acc_t[:rows] + acc_t[rows:]) * scale
    gap = acc_s - logits_t
    max_t = jnp.max(logits_t, axis=1, keepdims=True)
    max_s = jnp.max(acc_s, axis=1, keepdims=True)
    sum_t = jnp.sum(jnp.exp(logits_t - max_t), axis=1, keepdims=True)
    exp_s = jnp.exp(acc_s - max_s)
    sum_s = jnp.sum(exp_s, axis=1, keepdims=True)
    cross = jnp.sum(exp_s * gap, axis=1, keepdims=True) / sum_s
    me = d * n_t + t
    column = lax.broadcasted_iota(jnp.int32, (rows, vocab), 1) + me * vocab
    chosen = jnp.sum(
        jnp.where(column == wanted.astype(jnp.int32), gap, 0.0), axis=1, keepdims=True
    )

    place = lax.broadcasted_iota(jnp.int32, (rows, lanes), 1) - lax.broadcasted_iota(
        jnp.int32, (rows, lanes), 0
    )
    packed = jnp.zeros((rows, lanes), f32)
    for i, value in enumerate((max_t + jnp.log(sum_t), max_s + jnp.log(sum_s), cross, chosen)):
        packed = jnp.where(place == i * rows, value, packed)
    mine[...] = jnp.sum(packed, axis=0, keepdims=True)
    stats[me] = mine[...]

    def stat(k):
        peer = lax.rem(me + k, n_dev)
        return remote(
            mine, stats.at[me], st_send.at[k], st_recv.at[k], (peer // n_t, lax.rem(peer, n_t))
        )

    def start(k, carry):
        stat(k).start()
        return carry

    def finish(k, carry):
        stat(k).wait()
        return carry

    lax.fori_loop(1, n_dev, start, 0)
    for copy in started:
        copy.wait_send()
    lax.fori_loop(1, n_dev, finish, 0)

    table = stats[...].reshape(n_dev, lanes)
    top = jnp.max(table, axis=0, keepdims=True)
    weight = jnp.exp(table - top)
    total = jnp.sum(weight, axis=0, keepdims=True)
    lse = top + jnp.log(total)
    moved = pltpu.roll(weight, rows, 1)
    mean_gap = jnp.sum(table * moved, axis=0, keepdims=True) / jnp.sum(moved, axis=0, keepdims=True)
    target_gap = jnp.sum(table, axis=0, keepdims=True)

    def per_slot(value, i):
        return jnp.sum(jnp.where(place == i * rows, value, 0.0), axis=1, keepdims=True)

    lse_t, lse_s = per_slot(lse, 0), per_slot(lse, 1)
    mean = per_slot(mean_gap, 2)
    ratio = per_slot(target_gap, 3) - lse_s + lse_t
    kl = mean - lse_s + lse_t
    gradient = (exp_s * jnp.exp(max_s - lse_s) * (gap - mean)).astype(bf16)
    out_ref[...] = lax.dot_general(
        hit_bf16, gradient, (((0,), (0,)), ((), ())), preferred_element_type=f32
    ).astype(bf16)
    own_row = lax.broadcasted_iota(jnp.int32, (rows, local_tokens), 0) - d * LIVE
    own = (own_row == own_slot) & (own_slot >= 0)
    div_ref[...] = jnp.sum(jnp.where(own, kl, 0.0), axis=0, keepdims=True)
    ratio_ref[...] = jnp.sum(jnp.where(own, ratio, 0.0), axis=0, keepdims=True)


def on_device(
    teacher_hidden,
    student_hidden,
    teacher_head,
    student_head,
    teacher_gain,
    lengths,
    student_row,
    targets,
):
    n_dp = lax.axis_size("dp")
    n_t = lax.axis_size("tensor")
    local_tokens, width_t = teacher_hidden.shape
    width_s = student_hidden.shape[1]
    tokens = local_tokens * n_dp
    vocab = teacher_head.shape[1]
    rows = n_dp * LIVE
    half = n_t // 2
    n_dev = n_dp * n_t
    bf16, f32 = jnp.bfloat16, jnp.float32
    dma = pltpu.SemaphoreType.DMA
    hbm = pl.BlockSpec(memory_space=pl.ANY)
    vmem = pl.BlockSpec(memory_space=pltpu.VMEM)
    gradient, divergence, log_ratio = pl.pallas_call(
        functools.partial(kernel, n_dp, n_t),
        out_shape=(
            jax.ShapeDtypeStruct((tokens, vocab), bf16),
            jax.ShapeDtypeStruct((1, local_tokens), f32),
            jax.ShapeDtypeStruct((1, local_tokens), f32),
        ),
        in_specs=[hbm] * 8,
        out_specs=(vmem,) * 3,
        scratch_shapes=[
            pltpu.VMEM((local_tokens, width_t), bf16),
            pltpu.VMEM(teacher_head.shape, bf16),
            pltpu.VMEM(student_head.shape, bf16),
            pltpu.VMEM((n_t, 1, width_t), f32),
            pltpu.SMEM(lengths.shape, jnp.int32),
            pltpu.VMEM((1, tokens), jnp.int32),
            pltpu.VMEM((1, tokens), jnp.int32),
            pltpu.VMEM((n_t, n_dp, LIVE, width_t), bf16),
            pltpu.VMEM((n_dp, local_tokens, width_s), bf16),
            pltpu.VMEM((n_t, rows, width_s), bf16),
            pltpu.VMEM((1, 4 * rows), f32),
            pltpu.VMEM((n_dev, 1, 4 * rows), f32),
            dma((8,)),
            *[dma((n_dp,))] * 4,
            *[dma((half,))] * 8,
            *[dma((n_dev,))] * 2,
        ],
        compiler_params=pltpu.CompilerParams(collective_id=0, has_side_effects=True),
    )(
        teacher_hidden,
        student_hidden,
        teacher_head,
        student_head,
        teacher_gain.reshape(n_t, 1, width_t),
        lengths,
        student_row.reshape(1, tokens),
        targets.reshape(1, tokens),
    )
    return gradient, divergence.reshape(local_tokens), log_ratio.reshape(local_tokens)


def solution(mesh):
    return jax.shard_map(
        on_device,
        mesh=mesh,
        in_specs=(
            P("dp", "tensor"),
            P("dp", "tensor"),
            P(None, ("dp", "tensor")),
            P(None, ("dp", "tensor")),
            P(),
            P(),
            P(),
            P(),
        ),
        out_specs=(P(None, ("dp", "tensor")), P("dp"), P("dp")),
        check_vma=False,
    )
```

time: 116 us -> 25.8 us (0.22)
  blocking collectives: 94 us -> 0 us
  Pallas kernels: 0 us -> 21.3 us
  other arithmetic: 8.71 us -> 0 us
  local copies, waits for them, and re-layouts: 8.31 us -> 3.7 us
  matrix products: 3.05 us -> 0 us
    all_gather x4 -> x0, blocking collectives: 53.9 us -> none  [the longest x1 18.4 us: on_device(): lax.all_gather(teacher_full, 'dp', axis=0, tiled=True).astype(jnp.float32)]
    unnamed x1 -> x0, blocking collectives: 40.1 us -> none
    pallas_call x0 -> x1, Pallas kernels: none -> 21.3 us  [on_device(): pl.pallas_call(functools.partial(kernel, n_dp, n_t), out_shape=(jax.Shape...]
    mul x2 -> x0, other arithmetic: 5.08 us -> none  [the longest x1 5.07 us: on_device(): live_all * (picked_student - student_lse - (picked_teacher - teacher_lse))]
    gather x4 -> x0, local copies, waits for them, and re-layouts: 4.7 us -> none  [the longest x2 2.44 us: on_device(): chosen_rows = student_all[student_row[token_ids]]]
    dot_general x2 -> x0, matrix products: 3.05 us -> none  [the longest x1 2.34 us: on_device(): jnp.dot(chosen_rows, student_head, preferred_element_type=jnp.float32)]
    add x93 -> x0, other arithmetic: 2.35 us -> none  [the longest x31 0.98 us: combine(): earlier[1] * jnp.exp(earlier[0] - top_teacher)]
    unnamed x24 -> x3, local copies, waits for them, and re-layouts: 1.86 us -> 3.7 us
where the time goes in v1:
time: 25.8 us; the launch traced here: 25.6 us
  Pallas kernels  21.3 us (83%)
  local copies, waits for them, and re-layouts  3.7 us (14%)
  between operations  0.64 us (2%)
    pallas_call x1, Pallas kernels, on_device(): pl.pallas_call(functools.partial(kernel, n_dp, n_t), out_shape=(jax.Shape...  21.3 us
    unnamed x3, local copies, waits for them, and re-layouts  3.7 us

profile of v1, /device:TPU:0, one launch (start us, length us, event | category | flops | bytes accessed | tf_op | source)
XLA Modules:
  0.0 25.6 jit_solution(9511889376396716255)
XLA Ops:
  0.6 21.3 %shard_map.103 = (bf16[64,256]{1,0:T(8,128)(2,1)}, f32[1,16]{1,0:T(1,128)}, f32[1,16]{1,0:T(1,128)}) custom-call(bf16[16,640]{1,0:T(8,128)(2,1)} %th_hbm.1, bf16[16,512]{1,0:T(8,128)(2,1)} %sh_hbm.1, bf16[5120,256]{1,0:T(8,128)(2,1)} %thead_hbm.1, bf16[4096,256]{1,0:T(8,128)(2,1)} %shead_hbm.1, f32[8,1,640]{2,1,0:T(1,128)} %bitcast.5, s32[8]{0:T(128)} %len_hbm.1, ...), custom_call_target="tpu_custom_call" | custom-call | tf_op jit(solution)/shard_map/pallas_call | solution.py:312
  21.9 1.4 %copy.14 = bf16[64,256]{1,0:T(8,128)(2,1)} copy(bf16[64,256]{1,0:T(8,128)(2,1)} %get-tuple-element.12) | data formatting | bytes 65536
  23.3 1.2 %copy.15 = f32[16]{0:T(128)} copy(f32[16]{0:T(128)} %bitcast.9) | data formatting | bytes 128
  24.5 1.1 %copy.16 = f32[16]{0:T(128)} copy(f32[16]{0:T(128)} %bitcast.8) | data formatting | bytes 128

commit v2 on v1

--- a/solution.py
+++ b/solution.py
@@ -124,16 +124,30 @@
             src_ref=src, dst_ref=dst, send_sem=send, recv_sem=recv, device_id=device, device_id_type=MESH
         )
 
-    started = []
-    z_t, z_s = [], []
-    for k in range(1, n_dp):
-        z_t.append(
-            remote(tg.at[t, d], tg.at[t, d], zt_send.at[k], zt_recv.at[k], (dp_peer(k), t))
-        )
-        z_s.append(remote(sz.at[d], sz.at[d], zs_send.at[k], zs_recv.at[k], (dp_peer(k), t)))
-    for copy in z_t + z_s:
+    upper = (2 * d) // n_dp
+    order = [upper * m + (1 - upper) * (n_dp - m) for m in range(1, n_dp)]
+    z_s = [
+        remote(sz.at[d], sz.at[d], zs_send.at[k], zs_recv.at[k], (dp_peer(k), t)) for k in order
+    ]
+    z_t = [
+        remote(tg.at[t, d], tg.at[t, d], zt_send.at[k], zt_recv.at[k], (dp_peer(k), t))
+        for k in order
+    ]
+    for copy in z_s + z_t:
         copy.start()
-    started += z_t + z_s
+    started = z_s + z_t
+
+    def spread(j):
+        piece = tg.at[t, lax.rem(d - j + n_dp, n_dp)]
+        copies = [
+            remote(piece, piece, xt_send.at[k, j], xt_recv.at[k, j], (d, chip_peer(k)))
+            for k in range(1, half)
+        ]
+        for copy in copies:
+            copy.start()
+        return copies
+
+    x_t = [spread(0)]
 
     local[3].wait()
     local[4].wait()
@@ -154,16 +168,6 @@
     pick = lax.broadcasted_iota(jnp.int32, (rows, tokens), 1) == source.astype(jnp.int32)
     pick_bf16 = jnp.where(pick, 1.0, 0.0).astype(bf16)
 
-    for copy in z_t:
-        copy.wait_recv()
-    x_t = [
-        remote(tg.at[t], tg.at[t], xt_send.at[k], xt_recv.at[k], (d, chip_peer(k)))
-        for k in range(1, half)
-    ]
-    p_t = [remote(tg.at[t], tg.at[t], pt_send.at[0], pt_recv.at[0], (d, partner))]
-    for copy in x_t + p_t:
-        copy.start()
-
     for copy in z_s:
         copy.wait_recv()
     everyone = sz[...].reshape(tokens, width_s)
@@ -176,6 +180,12 @@
     for copy in x_s + p_s:
         copy.start()
 
+    for j, copy in zip(order, z_t):
+        copy.wait_recv()
+        x_t.append(spread(j))
+    p_t = [remote(tg.at[t], tg.at[t], pt_send.at[0], pt_recv.at[0], (d, partner))]
+    p_t[0].start()
+
     for copy in local[5:]:
         copy.wait()
 
@@ -183,39 +193,46 @@
     acc_t = jnp.zeros((2 * rows, vocab), f32)
     acc_s = jnp.zeros((rows, vocab), f32)
 
-    def add(which, square, acc_t, acc_s):
+    def add_t(which, square, acc_t):
         x = tg[which].astype(f32).reshape(rows, width_t)
         square = square + jnp.sum(x * x, axis=1, keepdims=True)
         x = x * gain[which]
         high = x.astype(bf16)
         low = (x - high.astype(f32)).astype(bf16)
         at_t = pl.ds(pl.multiple_of(which * width_t, width_t), width_t)
-        at_s = pl.ds(pl.multiple_of(which * width_s, width_s), width_s)
         acc_t = acc_t + jnp.dot(
             jnp.concatenate([high, low], axis=0), thead[at_t, :], preferred_element_type=f32
         )
-        acc_s = acc_s + jnp.dot(sg[which], shead[at_s, :], preferred_element_type=f32)
-        return square, acc_t, acc_s
-
-    sums = add(t, square, acc_t, acc_s)
+        return square, acc_t
+
+    def add_s(which, acc_s):
+        at_s = pl.ds(pl.multiple_of(which * width_s, width_s), width_s)
+        return acc_s + jnp.dot(sg[which], shead[at_s, :], preferred_element_type=f32)
+
+    same = [lax.rem(chip - k + half, half) * 2 + core for k in range(half)]
+    other = [lax.rem(chip - k + half, half) * 2 + 1 - core for k in range(half)]
+    square, acc_t = add_t(t, square, acc_t)
+    acc_s = add_s(t, acc_s)
     for k in range(1, half):
-        origin = lax.rem(chip - k + half, half) * 2 + core
-        x_t[k - 1].wait_recv()
-        copy = remote(tg.at[origin], tg.at[origin], pt_send.at[k], pt_recv.at[k], (d, partner))
-        copy.start()
-        p_t.append(copy)
+        for j, copies in zip([0] + order, x_t):
+            copies[k - 1].wait_recv()
+        block = tg.at[same[k]]
+        p_t.append(remote(block, block, pt_send.at[k], pt_recv.at[k], (d, partner)))
+        p_t[k].start()
         x_s[k - 1].wait_recv()
-        copy = remote(sg.at[origin], sg.at[origin], ps_send.at[k], ps_recv.at[k], (d, partner))
-        copy.start()
-        p_s.append(copy)
-        sums = add(origin, *sums)
+        block = sg.at[same[k]]
+        p_s.append(remote(block, block, ps_send.at[k], ps_recv.at[k], (d, partner)))
+        p_s[k].start()
+        square, acc_t = add_t(same[k], square, acc_t)
+        acc_s = add_s(same[k], acc_s)
     for k in range(half):
-        origin = lax.rem(chip - k + half, half) * 2 + 1 - core
         p_t[k].wait_recv()
         p_s[k].wait_recv()
-        sums = add(origin, *sums)
-    square, acc_t, acc_s = sums
-    started += x_t + x_s + p_t + p_s
+        square, acc_t = add_t(other[k], square, acc_t)
+        acc_s = add_s(other[k], acc_s)
+    for copies in x_t:
+        started += copies
+    started += x_s + p_t + p_s
 
     scale = lax.rsqrt(square / (width_t * n_t) + 1e-06)
     logits_t = (acc_t[:rows] + acc_t[rows:]) * scale
@@ -241,24 +258,24 @@
     mine[...] = jnp.sum(packed, axis=0, keepdims=True)
     stats[me] = mine[...]
 
-    def stat(k):
-        peer = lax.rem(me + k, n_dev)
-        return remote(
-            mine, stats.at[me], st_send.at[k], st_recv.at[k], (peer // n_t, lax.rem(peer, n_t))
-        )
-
-    def start(k, carry):
-        stat(k).start()
+    def stat(d_to, t_to):
+        remote(mine, stats.at[me], st_send.at[0], st_recv.at[0], (d_to, t_to)).start()
+
+    others = [lax.rem(t + j, n_t) for j in range(n_t)]
+
+    def start(m, carry):
+        d_to = dp_peer(upper * m + (1 - upper) * (n_dp - m))
+        for t_to in others:
+            stat(d_to, t_to)
         return carry
 
-    def finish(k, carry):
-        stat(k).wait()
-        return carry
-
-    lax.fori_loop(1, n_dev, start, 0)
+    lax.fori_loop(1, n_dp, start, 0, unroll=n_dp <= 4)
+    for t_to in others[1:]:
+        stat(d, t_to)
     for copy in started:
         copy.wait_send()
-    lax.fori_loop(1, n_dev, finish, 0)
+    rest = stats.at[pl.ds(0, n_dev - 1)]
+    remote(rest, rest, st_send.at[0], st_recv.at[0], (d, partner)).wait()
 
     table = stats[...].reshape(n_dev, lanes)
     top = jnp.max(table, axis=0, keepdims=True)
@@ -284,6 +301,17 @@
     own = (own_row == own_slot) & (own_slot >= 0)
     div_ref[...] = jnp.sum(jnp.where(own, kl, 0.0), axis=0, keepdims=True)
     ratio_ref[...] = jnp.sum(jnp.where(own, ratio, 0.0), axis=0, keepdims=True)
+
+
+def write_out(a, b, c, a_out, b_out, c_out, sem):
+    copies = [
+        pltpu.make_async_copy(src, dst, sem.at[i])
+        for i, (src, dst) in enumerate([(a, a_out), (b, b_out), (c, c_out)])
+    ]
+    for copy in copies:
+        copy.start()
+    for copy in copies:
+        copy.wait()
 
 
 def on_device(
@@ -312,9 +340,9 @@
     gradient, divergence, log_ratio = pl.pallas_call(
         functools.partial(kernel, n_dp, n_t),
         out_shape=(
-            jax.ShapeDtypeStruct((tokens, vocab), bf16),
-            jax.ShapeDtypeStruct((1, local_tokens), f32),
-            jax.ShapeDtypeStruct((1, local_tokens), f32),
+            pltpu.VMEM((tokens, vocab), bf16),
+            pltpu.VMEM((1, local_tokens), f32),
+            pltpu.VMEM((1, local_tokens), f32),
         ),
         in_specs=[hbm] * 8,
         out_specs=(vmem,) * 3,
@@ -333,8 +361,9 @@
             pltpu.VMEM((n_dev, 1, 4 * rows), f32),
             dma((8,)),
             *[dma((n_dp,))] * 4,
-            *[dma((half,))] * 8,
-            *[dma((n_dev,))] * 2,
+            *[dma((half, n_dp))] * 2,
+            *[dma((half,))] * 6,
+            *[dma((1,))] * 2,
         ],
         compiler_params=pltpu.CompilerParams(collective_id=0, has_side_effects=True),
     )(
@@ -347,6 +376,17 @@
         student_row.reshape(1, tokens),
         targets.reshape(1, tokens),
     )
+    gradient, divergence, log_ratio = pl.pallas_call(
+        write_out,
+        out_shape=(
+            jax.ShapeDtypeStruct((tokens, vocab), bf16),
+            jax.ShapeDtypeStruct((1, local_tokens), f32),
+            jax.ShapeDtypeStruct((1, local_tokens), f32),
+        ),
+        in_specs=[vmem] * 3,
+        out_specs=(hbm,) * 3,
+        scratch_shapes=[dma((3,))],
+    )(*[pltpu.with_memory_space_constraint(x, pltpu.VMEM) for x in (gradient, divergence, log_ratio)])
     return gradient, divergence.reshape(local_tokens), log_ratio.reshape(local_tokens)
 
 

time: 25.8 us -> 21.5 us (0.83)
  local copies, waits for them, and re-layouts: 3.7 us -> 0 us
  Pallas kernels: 21.3 us -> 20.7 us
    unnamed x3 -> x0, local copies, waits for them, and re-layouts: 3.7 us -> none
    pallas_call x1 -> x2, Pallas kernels: 21.3 us -> 20.7 us  [the longest x1 20 us: on_device(): pl.pallas_call(functools.partial(kernel, n_dp, n_t), out_shape=(pltpu.VME...]
where the time goes in v2:
time: 21.5 us; the launch traced here: 21.3 us
  Pallas kernels  20.7 us (96%)
  between operations  0.64 us (3%)
    pallas_call x1, Pallas kernels, on_device(): pl.pallas_call(functools.partial(kernel, n_dp, n_t), out_shape=(pltpu.VME...  20 us
    pallas_call x1, Pallas kernels, on_device(): pl.pallas_call(write_out, out_shape=(jax.ShapeDtypeStruct((tokens, vocab)...  0.65 us

profile of v2, /device:TPU:0, one launch (start us, length us, event | category | flops | bytes accessed | tf_op | source)
XLA Modules:
  0.0 21.3 jit_solution(10307950388865532022)
XLA Ops:
  0.6 20.0 %shard_map.103 = (bf16[64,256]{1,0:T(8,128)(2,1)S(1)}, f32[1,16]{1,0:T(1,128)S(1)}, f32[1,16]{1,0:T(1,128)S(1)}) custom-call(bf16[16,640]{1,0:T(8,128)(2,1)} %th_hbm.1, bf16[16,512]{1,0:T(8,128)(2,1)} %sh_hbm.1, bf16[5120,256]{1,0:T(8,128)(2,1)} %thead_hbm.1, bf16[4096,256]{1,0:T(8,128)(2,1)} %shead_hbm.1, f32[8,1,640]{2,1,0:T(1,128)} %bitcast.5, s32[8]{0:T(128)} %len_hbm.1, ...), custom_call_target="tpu_custom_call" | custom-call | tf_op jit(solution)/shard_map/pallas_call | solution.py:340
  20.7 0.6 %shard_map.104 = (bf16[64,256]{1,0:T(8,128)(2,1)}, f32[1,16]{1,0:T(1,128)}, f32[1,16]{1,0:T(1,128)}) custom-call(bf16[64,256]{1,0:T(8,128)(2,1)S(1)} %get-tuple-element.9.a, f32[1,16]{1,0:T(1,128)S(1)} %get-tuple-element.10.b, f32[1,16]{1,0:T(1,128)S(1)} %get-tuple-element.11.c), custom_call_target="tpu_custom_call" | custom-call | tf_op jit(solution)/shard_map/pallas_call | solution.py:379

commit v3 on v2

--- a/solution.py
+++ b/solution.py
@@ -70,6 +70,26 @@
     lanes = 4 * rows
     n_dev = n_dp * n_t
 
+    def dp_peer(k):
+        return lax.rem(d + k, n_dp)
+
+    turn = lax.rem(2 * half - 1 - 2 * chip + half * half, half)
+
+    def chip_at(k):
+        return lax.rem(chip + turn * k, half)
+
+    def chip_peer(k):
+        return chip_at(k) * 2 + core
+
+    barrier = pltpu.get_barrier_semaphore()
+    upper = (2 * d) // n_dp
+    order = [upper * m + (1 - upper) * (n_dp - m) for m in range(1, n_dp)]
+    for k in order:
+        pl.semaphore_signal(barrier, inc=1, device_id=(dp_peer(k), t), device_id_type=MESH)
+    for k in range(1, half):
+        pl.semaphore_signal(barrier, inc=1, device_id=(d, chip_peer(k)), device_id_type=MESH)
+    pl.semaphore_signal(barrier, inc=1, device_id=(d, partner), device_id_type=MESH)
+
     local = [
         pltpu.make_async_copy(src, dst, local_sem.at[i])
         for i, (src, dst) in enumerate(
@@ -88,19 +108,6 @@
     for copy in local:
         copy.start()
 
-    def dp_peer(k):
-        return lax.rem(d + k, n_dp)
-
-    def chip_peer(k):
-        return lax.rem(chip + k, half) * 2 + core
-
-    barrier = pltpu.get_barrier_semaphore()
-    for k in range(1, n_dp):
-        pl.semaphore_signal(barrier, inc=1, device_id=(dp_peer(k), t), device_id_type=MESH)
-    for k in range(1, half):
-        pl.semaphore_signal(barrier, inc=1, device_id=(d, chip_peer(k)), device_id_type=MESH)
-    pl.semaphore_signal(barrier, inc=1, device_id=(d, partner), device_id_type=MESH)
-
     local[0].wait()
     lane = lax.broadcasted_iota(jnp.int32, (1, local_tokens), 1)
     own_slot = jnp.full((1, local_tokens), -1, jnp.int32)
@@ -124,8 +131,6 @@
             src_ref=src, dst_ref=dst, send_sem=send, recv_sem=recv, device_id=device, device_id_type=MESH
         )
 
-    upper = (2 * d) // n_dp
-    order = [upper * m + (1 - upper) * (n_dp - m) for m in range(1, n_dp)]
     z_s = [
         remote(sz.at[d], sz.at[d], zs_send.at[k], zs_recv.at[k], (dp_peer(k), t)) for k in order
     ]
@@ -140,7 +145,7 @@
     def spread(j):
         piece = tg.at[t, lax.rem(d - j + n_dp, n_dp)]
         copies = [
-            remote(piece, piece, xt_send.at[k, j], xt_recv.at[k, j], (d, chip_peer(k)))
+            remote(piece, piece, xt_send.at[k, j], xt_recv.at[chip, j], (d, chip_peer(k)))
             for k in range(1, half)
         ]
         for copy in copies:
@@ -168,21 +173,24 @@
     pick = lax.broadcasted_iota(jnp.int32, (rows, tokens), 1) == source.astype(jnp.int32)
     pick_bf16 = jnp.where(pick, 1.0, 0.0).astype(bf16)
 
+    for j, copy in zip(order[:-1], z_t[:-1]):
+        copy.wait_recv()
+        x_t.append(spread(j))
+
     for copy in z_s:
         copy.wait_recv()
     everyone = sz[...].reshape(tokens, width_s)
     sg[t] = jnp.dot(pick_bf16, everyone, preferred_element_type=f32).astype(bf16)
     x_s = [
-        remote(sg.at[t], sg.at[t], xs_send.at[k], xs_recv.at[k], (d, chip_peer(k)))
+        remote(sg.at[t], sg.at[t], xs_send.at[k], xs_recv.at[chip], (d, chip_peer(k)))
         for k in range(1, half)
     ]
     p_s = [remote(sg.at[t], sg.at[t], ps_send.at[0], ps_recv.at[0], (d, partner))]
     for copy in x_s + p_s:
         copy.start()
 
-    for j, copy in zip(order, z_t):
-        copy.wait_recv()
-        x_t.append(spread(j))
+    z_t[-1].wait_recv()
+    x_t.append(spread(order[-1]))
     p_t = [remote(tg.at[t], tg.at[t], pt_send.at[0], pt_recv.at[0], (d, partner))]
     p_t[0].start()
 
@@ -209,27 +217,31 @@
         at_s = pl.ds(pl.multiple_of(which * width_s, width_s), width_s)
         return acc_s + jnp.dot(sg[which], shead[at_s, :], preferred_element_type=f32)
 
-    same = [lax.rem(chip - k + half, half) * 2 + core for k in range(half)]
-    other = [lax.rem(chip - k + half, half) * 2 + 1 - core for k in range(half)]
     square, acc_t = add_t(t, square, acc_t)
     acc_s = add_s(t, acc_s)
+    pieces = [0] + order
     for k in range(1, half):
-        for j, copies in zip([0] + order, x_t):
-            copies[k - 1].wait_recv()
-        block = tg.at[same[k]]
+        origin = chip_at(half - k)
+        block = tg.at[origin * 2 + core]
+        for j in pieces:
+            piece = tg.at[origin * 2 + core, lax.rem(d - j + n_dp, n_dp)]
+            remote(
+                piece, piece, xt_send.at[k, j], xt_recv.at[origin, j], (d, partner)
+            ).wait_recv()
         p_t.append(remote(block, block, pt_send.at[k], pt_recv.at[k], (d, partner)))
         p_t[k].start()
-        x_s[k - 1].wait_recv()
-        block = sg.at[same[k]]
+        block = sg.at[origin * 2 + core]
+        remote(block, block, xs_send.at[k], xs_recv.at[origin], (d, partner)).wait_recv()
         p_s.append(remote(block, block, ps_send.at[k], ps_recv.at[k], (d, partner)))
         p_s[k].start()
-        square, acc_t = add_t(same[k], square, acc_t)
-        acc_s = add_s(same[k], acc_s)
+        square, acc_t = add_t(origin * 2 + core, square, acc_t)
+        acc_s = add_s(origin * 2 + core, acc_s)
     for k in range(half):
+        origin = chip_at(half - k) if k else chip
         p_t[k].wait_recv()
         p_s[k].wait_recv()
-        square, acc_t = add_t(other[k], square, acc_t)
-        acc_s = add_s(other[k], acc_s)
+        square, acc_t = add_t(origin * 2 + 1 - core, square, acc_t)
+        acc_s = add_s(origin * 2 + 1 - core, acc_s)
     for copies in x_t:
         started += copies
     started += x_s + p_t + p_s

time: 21.5 us -> 21.1 us (0.981)
  Pallas kernels: 20.7 us -> 20.3 us
    pallas_call x1, Pallas kernels: 20 us -> 19.7 us  [on_device(): pl.pallas_call(functools.partial(kernel, n_dp, n_t), out_shape=(pltpu.VME...]
where the time goes in v3:
time: 21.1 us; the launch traced here: 21 us
  Pallas kernels  20.3 us (96%)
  between operations  0.64 us (3%)
    pallas_call x1, Pallas kernels, on_device(): pl.pallas_call(functools.partial(kernel, n_dp, n_t), out_shape=(pltpu.VME...  19.7 us
    pallas_call x1, Pallas kernels, on_device(): pl.pallas_call(write_out, out_shape=(jax.ShapeDtypeStruct((tokens, vocab)...  0.65 us

profile of v3, /device:TPU:0, one launch (start us, length us, event | category | flops | bytes accessed | tf_op | source)
XLA Modules:
  0.0 21.0 jit_solution(11224410702918862450)
XLA Ops:
  0.6 19.7 %shard_map.103 = (bf16[64,256]{1,0:T(8,128)(2,1)S(1)}, f32[1,16]{1,0:T(1,128)S(1)}, f32[1,16]{1,0:T(1,128)S(1)}) custom-call(bf16[16,640]{1,0:T(8,128)(2,1)} %th_hbm.1, bf16[16,512]{1,0:T(8,128)(2,1)} %sh_hbm.1, bf16[5120,256]{1,0:T(8,128)(2,1)} %thead_hbm.1, bf16[4096,256]{1,0:T(8,128)(2,1)} %shead_hbm.1, f32[8,1,640]{2,1,0:T(1,128)} %bitcast.5, s32[8]{0:T(128)} %len_hbm.1, ...), custom_call_target="tpu_custom_call" | custom-call | tf_op jit(solution)/shard_map/pallas_call | solution.py:352
  20.3 0.6 %shard_map.104 = (bf16[64,256]{1,0:T(8,128)(2,1)}, f32[1,16]{1,0:T(1,128)}, f32[1,16]{1,0:T(1,128)}) custom-call(bf16[64,256]{1,0:T(8,128)(2,1)S(1)} %get-tuple-element.9.a, f32[1,16]{1,0:T(1,128)S(1)} %get-tuple-element.10.b, f32[1,16]{1,0:T(1,128)S(1)} %get-tuple-element.11.c), custom_call_target="tpu_custom_call" | custom-call | tf_op jit(solution)/shard_map/pallas_call | solution.py:391
